TPU v7x, 512 devices: a whole 4x8x8 slice. The times are simulated.
512 devices in a mesh: grp: 8 (over z_hi, core), shard: 64 (over z_lo, y, x).
Axes of the slice: x: 4, y: 8, z: 8 (z_hi: 4, z_lo: 2; z = z_hi * 2 + z_lo), core: 2. Of those that a mesh axis runs over, the one named last changes fastest.
Arguments:
- gradients: float32 [8, 1024, 512], P('grp', 'shard'), may hold values from -6 to 6
- weight: float32 [1024, 512], P('shard'), may hold values from -0.1875 to 0.1875
- moment: float32 [1024, 512], P('shard'), may hold values from -4 to 4
- second: float32 [1024, 512], P('shard'), may hold values from 0.01 to 0.5
- left_gram: float32 [1024, 1024], P('shard'), may hold values from -3 to 60, as said below
- left_basis: float32 [1024, 1024], P('shard'), may hold values from -0.1 to 1.1, as said below
- right_gram: float32 [512, 512], P('shard'), may hold values from -3 to 60, as said below
- right_basis: float32 [512, 512], P('shard'), may hold values from -0.1 to 1.1, as said below
Outputs:
- weight_new: float32 [1024, 512], P('shard')
- moment_new: float32 [1024, 512], P('shard')
- second_new: float32 [1024, 512], P('shard')
- left_new: float32 [1024, 1024], P('shard')
- left_basis_new: float32 [1024, 1024], P('shard')
- right_new: float32 [512, 512], P('shard')
- right_basis_new: float32 [512, 512], P('shard')
Inputs may be any that keep to these rules, and one draw needn't show every extreme that they name: `left_gram`: symmetric positive definite. `right_gram`: symmetric positive definite. `left_basis`: square and of full rank. `right_basis`: square and of full rank.
All inputs are finite; a program needn't handle non-finite values.
Results may differ from a plain program's by a relative error of at most 0.0015.
The roundings to bfloat16 on the way count: a program that leaves them out, or rounds other values in their place, can miss the bound.
Values may be sent and summed in bfloat16 or wider, within the bound.
No kernel may reach another device: no remote copies, remote signals or barrier semaphores. Data moves between devices by JAX's collectives and lax.ppermute only.
A program may use at most 64 MiB of HBM per device.

v0:
```python
import jax
import jax.numpy as jnp
from jax import lax
from jax.sharding import PartitionSpec as P

NS_ITERS = 2
BETA_ONE = 0.9
BETA_TWO = 0.95
GRAM_DECAY = 0.95
ADAM_EPS = 1e-08
NORM_EPS = 1e-06
STEP_SIZE = 0.02
START_SCALE = 0.75
PRECISE = lax.Precision.HIGHEST


def inner_rows(former, latter):
    return lax.dot_general(
        former, latter, (((0,), (0,)), ((), ())), preferred_element_type=jnp.float32
    )


def outer_rows(former, latter):
    return lax.dot_general(
        former, latter, (((1,), (1,)), ((), ())), preferred_element_type=jnp.float32
    )


def start_rows(power_rows, column_sums):
    scaled = START_SCALE * power_rows / jnp.sqrt(column_sums + NORM_EPS)
    return lax.optimization_barrier(scaled.astype(jnp.bfloat16))


def left_sweep(current):
    segment = lax.all_gather(current, "shard", axis=0, tiled=True)
    square = outer_rows(current, segment).astype(jnp.bfloat16)
    running = jnp.dot(square, segment, preferred_element_type=jnp.float32)
    return 1.5 * current.astype(jnp.float32) - 0.5 * running


def right_sweep(current):
    segment = lax.all_gather(current, "shard", axis=0, tiled=True)
    square = outer_rows(current, segment).astype(jnp.bfloat16)
    running = jnp.dot(square, segment, preferred_element_type=jnp.float32)
    return 1.5 * current.astype(jnp.float32) - 0.5 * running


def local(gradients, weight, moment, second, left_gram, left_basis, right_gram, right_basis):
    local_rows = weight.shape[0]
    right_rows = right_gram.shape[0]
    row_first = lax.axis_index("shard") * local_rows
    right_first = lax.axis_index("shard") * right_rows
    gradient = lax.psum(gradients[0], "grp") / lax.axis_size("grp")
    moment_new = BETA_ONE * moment + (1.0 - BETA_ONE) * gradient
    grad_half = gradient.astype(jnp.bfloat16)
    moment_half = moment_new.astype(jnp.bfloat16)
    left_half = left_basis.astype(jnp.bfloat16)
    right_whole = lax.all_gather(right_basis.astype(jnp.bfloat16), "shard", axis=0, tiled=True)
    right_wide = lax.optimization_barrier(right_whole).astype(jnp.float32)
    basis_part = lax.all_gather(left_half, "shard", axis=0, tiled=True)
    grad_part = lax.all_gather(grad_half, "shard", axis=0, tiled=True)
    basis_columns = lax.dynamic_slice_in_dim(basis_part, row_first, local_rows, 1)
    turned = inner_rows(basis_columns, grad_part)
    gram_block = GRAM_DECAY * left_gram + (1.0 - GRAM_DECAY) * outer_rows(grad_half, grad_part)
    power_rows = jnp.dot(gram_block, basis_part.astype(jnp.float32), precision=PRECISE)
    grad_columns = lax.dynamic_slice_in_dim(grad_part, right_first, right_rows, 1)
    right_terms = inner_rows(grad_columns, grad_part)
    core_state, basis_columns = ((turned, gram_block, power_rows, right_terms), basis_columns)
    core_state, turned_moment = (
        core_state,
        inner_rows(basis_columns, lax.all_gather(moment_half, "shard", axis=0, tiled=True)),
    )
    turned_grad, left_new, left_power, right_terms = core_state
    right_new = GRAM_DECAY * right_gram + (1.0 - GRAM_DECAY) * right_terms
    rotated_grad = jnp.dot(
        turned_grad.astype(jnp.bfloat16), right_whole, preferred_element_type=jnp.float32
    )
    rotated_moment = jnp.dot(
        turned_moment.astype(jnp.bfloat16), right_whole, preferred_element_type=jnp.float32
    )
    second_new = BETA_TWO * second + (1.0 - BETA_TWO) * rotated_grad * rotated_grad
    direction = (rotated_moment / (jnp.sqrt(second_new) + ADAM_EPS)).astype(jnp.bfloat16)
    returned = outer_rows(direction, right_whole).astype(jnp.bfloat16)
    update = jnp.dot(
        left_half,
        lax.all_gather(returned, "shard", axis=0, tiled=True),
        preferred_element_type=jnp.float32,
    )
    weight_new = weight - STEP_SIZE * update
    right_power = jnp.dot(right_new, right_wide, precision=PRECISE)
    left_sums, right_sums = lax.psum(
        (jnp.sum(left_power * left_power, axis=0), jnp.sum(right_power * right_power, axis=0)),
        "shard",
    )
    right_current = start_rows(right_power, right_sums)
    right_result = right_power
    for sweep in range(NS_ITERS):
        right_result = right_sweep(right_current)
        right_current = lax.optimization_barrier(right_result.astype(jnp.bfloat16))
    left_current = start_rows(left_power, left_sums)
    left_result = left_power
    for sweep in range(NS_ITERS):
        left_result = left_sweep(left_current)
        left_current = lax.optimization_barrier(left_result.astype(jnp.bfloat16))
    return (weight_new, moment_new, second_new, left_new, left_result, right_new, right_result)


def solution(mesh):
    return jax.shard_map(
        local,
        mesh=mesh,
        in_specs=(
            P("grp", "shard", None),
            P("shard", None),
            P("shard", None),
            P("shard", None),
            P("shard", None),
            P("shard", None),
            P("shard", None),
            P("shard", None),
        ),
        out_specs=(
            P("shard", None),
            P("shard", None),
            P("shard", None),
            P("shard", None),
            P("shard", None),
            P("shard", None),
            P("shard", None),
        ),
        check_vma=False,
    )
```

profile of v0, /device:TPU:2, one launch (start us, length us, event | category | flops | bytes accessed | tf_op | source)
XLA Modules:
  0.0 1857.0 jit_solution(10023106520451230898)
XLA Ops:
  7.2 0.0 copy-start.8
  7.2 0.0 all-gather.11.cloned.1.call-start
  7.2 36.2 %psum.21 = f32[16,512]{1,0:T(8,128)S(1)} all-reduce(f32[16,512]{1,0:T(8,128)} %bitcast.32), channel_id=1, replica_groups=mesh['grp'=8,'shard'=64] {'grp'}, use_global_device_ids=true, to_apply=%region_0.0 | all-reduce | flops 8192 | bytes 65536 | tf_op jit(solution)/shard_map/psum | solution.py:53
  43.4 1.4 fusion.29
  44.8 0.0 all-gather.11.cloned.1.call-update
  44.8 0.0 all-gather.7.cloned.1.call-start
  44.9 1.5 convert_element_type.62
  46.3 0.0 all-gather.7.cloned.1.call-update
  46.4 0.0 all-gather.9.cloned.1.call-start
  46.4 0.7 all-gather.9.cloned.1.call-update
  47.1 0.0 all-gather.15.cloned.1.call-start
  47.1 0.7 convert_element_type.65
  47.9 154.5 %all_gather.29 = bf16[512,512]{1,0:T(8,128)(2,1)S(1)} all-gather(bf16[8,512]{1,0:T(8,128)(2,1)S(1)} %convert_element_type.65), channel_id=1, replica_groups=mesh['grp'=8,'shard'=64] {'shard'}, dimensions={0}, use_global_device_ids=true | all-gather | bytes 532480 | tf_op jit(solution)/shard_map/all_gather | solution.py:58
  202.3 138.1 %all-gather.11.cloned.1.call-done = bf16[1024,512]{1,0:T(8,128)(2,1)} async-done(((bf16[16,512]{1,0:T(8,128)(2,1)}), bf16[1024,512]{1,0:T(8,128)(2,1)}) %all-gather.11.cloned.1.call-update) | async-done | bytes 1048592 | tf_op jit(solution)/shard_map/all_gather | solution.py:61
  340.4 1.7 fusion.8
  342.1 0.3 multiply_reduce_fusion.1
  342.4 0.0 copy-done.8
  342.4 0.0 copy-done.5
  342.4 1.6 fusion.2
  344.0 0.0 copy-start
  344.1 0.0 copy-start.9
  344.1 298.7 %all-gather.7.cloned.1.call-done = bf16[1024,1024]{1,0:T(8,128)(2,1)} async-done(((bf16[16,1024]{1,0:T(8,128)(2,1)}), bf16[1024,1024]{1,0:T(8,128)(2,1)}) %all-gather.7.cloned.1.call-update) | async-done | bytes 2097168 | tf_op jit(solution)/shard_map/all_gather | solution.py:60
  642.8 2.5 multiply_reduce_fusion
  645.4 156.0 %all-reduce = (f32[1024]{0:T(1024)S(1)}, f32[512]{0:T(512)S(1)}) all-reduce(f32[1024]{0:T(1024)S(1)} %get-tuple-element.12, f32[512]{0:T(512)S(1)} %get-tuple-element.14), channel_id=1, replica_groups=mesh['grp'=8,'shard'=64] {'shard'}, use_global_device_ids=true, to_apply=%region_2.0 | all-reduce | flops 1536 | bytes 12288 | tf_op jit(solution)/shard_map/psum | solution.py:91
  801.3 0.6 divide_convert_fusion
  802.0 0.0 all-gather.15.cloned.1.call-update
  802.0 0.0 all-gather.13.cloned.1.call-start
  802.0 0.0 copy-start.2
  802.1 140.5 %all-gather.9.cloned.1.call-done = bf16[1024,512]{1,0:T(8,128)(2,1)} async-done(((bf16[16,512]{1,0:T(8,128)(2,1)}), bf16[1024,512]{1,0:T(8,128)(2,1)}) %all-gather.9.cloned.1.call-update) | async-done | bytes 1048592 | tf_op jit(solution)/shard_map/all_gather | solution.py:71
  942.6 1.7 convolution_convert_fusion.3
  944.3 0.0 copy-done
  944.3 0.0 copy-done.9
  944.3 1.5 fusion.18
  945.8 0.0 copy-start.6
  945.8 1.0 convolution_convert_fusion.4
  946.8 0.0 all-gather.13.cloned.1.call-update
  946.8 0.0 all-gather.17.cloned.1.call-start
  946.8 298.1 %all-gather.15.cloned.1.call-done = bf16[1024,1024]{1,0:T(8,128)(2,1)} async-done(((bf16[16,1024]{1,0:T(8,128)(2,1)}), bf16[1024,1024]{1,0:T(8,128)(2,1)}) %all-gather.15.cloned.1.call-update) | async-done | bytes 2097168 | tf_op jit(solution)/shard_map/all_gather | solution.py:35
  1244.9 3.8 fusion.3
  1248.7 0.0 all-gather.17.cloned.1.call-update
  1248.8 0.0 copy-start.1
  1248.8 154.3 %all_gather.34 = bf16[512,512]{1,0:T(8,128)(2,1)S(1)} all-gather(bf16[8,512]{1,0:T(8,128)(2,1)S(1)} %divide_convert_fusion.1), channel_id=1, replica_groups=mesh['grp'=8,'shard'=64] {'shard'}, dimensions={0}, use_global_device_ids=true | all-gather | bytes 532480 | tf_op jit(solution)/shard_map/all_gather | solution.py:42
  1403.1 0.4 fusion.11
  1403.5 157.4 %all_gather.35 = bf16[512,512]{1,0:T(8,128)(2,1)S(1)} all-gather(bf16[8,512]{1,0:T(8,128)(2,1)S(1)} %fusion.11), channel_id=1, replica_groups=mesh['grp'=8,'shard'=64] {'shard'}, dimensions={0}, use_global_device_ids=true | all-gather | bytes 532480 | tf_op jit(solution)/shard_map/all_gather | solution.py:42
  1560.9 1.0 fusion.9
  1561.9 2.1 fusion.5
  1564.0 282.3 %all-gather.17.cloned.1.call-done = bf16[1024,1024]{1,0:T(8,128)(2,1)} async-done(((bf16[16,1024]{1,0:T(8,128)(2,1)}), bf16[1024,1024]{1,0:T(8,128)(2,1)}) %all-gather.17.cloned.1.call-update) | async-done | bytes 2097168 | tf_op jit(solution)/shard_map/all_gather | solution.py:35
  1846.3 3.8 fusion
  (16 shorter events, 0.0 us)
Async XLA Ops:
  7.2 335.3 %copy-start.8 = (f32[16,1024]{1,0:T(8,128)S(1)}, f32[16,1024]{1,0:T(8,128)}, u32[]{:S(2)}) copy-start(f32[16,1024]{1,0:T(8,128)} %param.12) | copy-start | bytes 196612
  7.2 333.2 %all-gather.11.cloned.1.call-start = ((), (), s32[]{:S(2)}) async-start(), calls=%async_computation.2 | async-start | bytes 1064960 | tf_op jit(solution)/shard_map/all_gather | solution.py:61
  44.8 297.6 %copy-start.5 = (bf16[16,512]{1,0:T(8,128)(2,1)S(1)}, bf16[16,512]{1,0:T(8,128)(2,1)}, u32[]{:S(2)}) copy-start(bf16[16,512]{1,0:T(8,128)(2,1)} %get-tuple-element.11) | copy-start | bytes 49156
  44.8 598.0 %all-gather.7.cloned.1.call-start = ((), (), s32[]{:S(2)}) async-start(), calls=%async_computation | async-start | bytes 2129920 | tf_op jit(solution)/shard_map/all_gather | solution.py:60
  46.4 896.2 %all-gather.9.cloned.1.call-start = ((), (), s32[]{:S(2)}) async-start(), calls=%async_computation.1 | async-start | bytes 1064960 | tf_op jit(solution)/shard_map/all_gather | solution.py:71
  47.1 1197.8 %all-gather.15.cloned.1.call-start = ((), (), s32[]{:S(2)}) async-start(), calls=%async_computation.4 | async-start | bytes 2129920 | tf_op jit(solution)/shard_map/all_gather | solution.py:35
  342.1 602.2 %copy-start.7 = (f32[8,512]{1,0:T(8,128)}, f32[8,512]{1,0:T(8,128)S(1)}, u32[]{:S(2)}) copy-start(f32[8,512]{1,0:T(8,128)S(1)} %fusion.8) | copy-start | bytes 49156
  344.0 601.7 %copy-start.4 = (f32[16,1024]{1,0:T(8,128)}, f32[16,1024]{1,0:T(8,128)S(1)}, u32[]{:S(2)}) copy-start(f32[16,1024]{1,0:T(8,128)S(1)} %fusion.2) | copy-start | bytes 196612
  344.0 600.2 %copy-start = (bf16[1024,512]{1,0:T(8,128)(2,1)S(1)}, bf16[1024,512]{1,0:T(8,128)(2,1)}, u32[]{:S(2)}) copy-start(bf16[1024,512]{1,0:T(8,128)(2,1)} %all-gather.11.cloned.1.call-done) | copy-start | bytes 3145732
  344.1 600.2 %copy-start.9 = (f32[16,512]{1,0:T(8,128)S(1)}, f32[16,512]{1,0:T(8,128)}, u32[]{:S(2)}) copy-start(f32[16,512]{1,0:T(8,128)} %param.11) | copy-start | bytes 98308
  802.0 759.9 %all-gather.13.cloned.1.call-start = ((), (), s32[]{:S(2)}) async-start(), calls=%async_computation.3 | async-start | bytes 1064960 | tf_op jit(solution)/shard_map/all_gather | solution.py:86
  802.0 442.9 %copy-start.2 = (bf16[16,1024]{1,0:T(8,128)(2,1)S(1)}, bf16[16,1024]{1,0:T(8,128)(2,1)}, u32[]{:S(2)}) copy-start(bf16[16,1024]{1,0:T(8,128)(2,1)} %divide_convert_fusion) | copy-start | bytes 98308
  945.8 303.0 %copy-start.6 = (f32[16,512]{1,0:T(8,128)}, f32[16,512]{1,0:T(8,128)S(1)}, u32[]{:S(2)}) copy-start(f32[16,512]{1,0:T(8,128)S(1)} %fusion.18) | copy-start | bytes 98308
  946.8 899.6 %all-gather.17.cloned.1.call-start = ((), (), s32[]{:S(2)}) async-start(), calls=%async_computation.5 | async-start | bytes 2129920 | tf_op jit(solution)/shard_map/all_gather | solution.py:35
  1248.7 313.2 %copy-start.3 = (bf16[16,1024]{1,0:T(8,128)(2,1)S(1)}, bf16[16,1024]{1,0:T(8,128)(2,1)}, u32[]{:S(2)}) copy-start(bf16[16,1024]{1,0:T(8,128)(2,1)} %convert_element_type.62) | copy-start | bytes 98308
  1248.7 313.2 %copy-start.10 = (f32[16,512]{1,0:T(8,128)S(1)}, f32[16,512]{1,0:T(8,128)}, u32[]{:S(2)}) copy-start(f32[16,512]{1,0:T(8,128)} %param.9) | copy-start | bytes 98308
  1248.8 597.6 %copy-start.1 = (bf16[16,1024]{1,0:T(8,128)(2,1)S(1)}, bf16[16,1024]{1,0:T(8,128)(2,1)}, u32[]{:S(2)}) copy-start(bf16[16,1024]{1,0:T(8,128)(2,1)} %fusion.3) | copy-start | bytes 98308
Sparse Core Ops, SparseCore 0:
  44.9 295.3 all-gather.10
  343.0 299.7 all-gather.6
  645.5 297.0 all-gather.8
  945.1 299.8 all-gather.14
  1246.9 297.0 all-gather.12
  1546.5 299.7 all-gather.16
where the time goes:
time: 1860 us
  waiting for transfers between devices  1160 us (62%)
  blocking collectives  658 us (35%)
  matrix products  21.4 us (1%)
    all_gather x2, waiting for transfers between devices, left_sweep(): segment = lax.all_gather(current, 'shard', axis=0, tiled=True)  580 us
    all_gather x2, blocking collectives, right_sweep(): segment = lax.all_gather(current, 'shard', axis=0, tiled=True)  312 us
    all_gather x1, waiting for transfers between devices, local(): basis_part = lax.all_gather(left_half, 'shard', axis=0, tiled=True)  299 us
    psum x1, blocking collectives, local(): lax.psum((jnp.sum(left_power * left_power, axis=0), jnp.sum(right_power *...  156 us
    all_gather x1, blocking collectives, local(): lax.all_gather(right_basis.astype(jnp.bfloat16), 'shard', axis=0, tiled=T...  154 us
    all_gather x1, waiting for transfers between devices, local(): lax.all_gather(moment_half, 'shard', axis=0, tiled=True)  141 us
    all_gather x1, waiting for transfers between devices, local(): grad_part = lax.all_gather(grad_half, 'shard', axis=0, tiled=True)  138 us
  transfers between devices with their start and end apart: 6, of which 5 were waited for; matrix products, arithmetic and copies ran while one was open for 1% of the time, Pallas kernels for 0%

commit v1 on v0

--- a/solution.py
+++ b/solution.py
@@ -57,8 +57,9 @@
     left_half = left_basis.astype(jnp.bfloat16)
     right_whole = lax.all_gather(right_basis.astype(jnp.bfloat16), "shard", axis=0, tiled=True)
     right_wide = lax.optimization_barrier(right_whole).astype(jnp.float32)
-    basis_part = lax.all_gather(left_half, "shard", axis=0, tiled=True)
-    grad_part = lax.all_gather(grad_half, "shard", axis=0, tiled=True)
+    value_now = jnp.concatenate([left_half, grad_half], axis=1)
+    out_arr = jax.lax.all_gather(value_now, "shard", axis=0, tiled=True)
+    basis_part, grad_part = jnp.split(out_arr, [left_half.shape[1]], axis=1)
     basis_columns = lax.dynamic_slice_in_dim(basis_part, row_first, local_rows, 1)
     turned = inner_rows(basis_columns, grad_part)
     gram_block = GRAM_DECAY * left_gram + (1.0 - GRAM_DECAY) * outer_rows(grad_half, grad_part)

time: 1860 us -> 1560 us (0.84)
  waiting for transfers between devices: 1160 us -> 860 us
    all_gather x2 -> x1, waiting for transfers between devices: 437 us -> 145 us  [local(): out_arr = jax.lax.all_gather(value_now, 'shard', axis=0, tiled=True)]
  transfers between devices with their start and end apart: 6 -> 5, of which waited for: 5 -> 4; matrix products, arithmetic and copies ran while one was open for 1% -> 1% of each run, Pallas kernels for 0% -> 0%
where the time goes in v1:
time: 1560 us
  waiting for transfers between devices  860 us (55%)
  blocking collectives  659 us (42%)
  matrix products  19.9 us (1%)
    all_gather x2, waiting for transfers between devices, left_sweep(): segment = lax.all_gather(current, 'shard', axis=0, tiled=True)  579 us
    all_gather x2, blocking collectives, right_sweep(): segment = lax.all_gather(current, 'shard', axis=0, tiled=True)  312 us
    psum x1, blocking collectives, local(): lax.psum((jnp.sum(left_power * left_power, axis=0), jnp.sum(right_power *...  156 us
    all_gather x1, blocking collectives, local(): lax.all_gather(right_basis.astype(jnp.bfloat16), 'shard', axis=0, tiled=T...  155 us
    all_gather x1, waiting for transfers between devices, local(): out_arr = jax.lax.all_gather(value_now, 'shard', axis=0, tiled=True)  145 us
    all_gather x1, waiting for transfers between devices, local(): lax.all_gather(moment_half, 'shard', axis=0, tiled=True)  135 us
    psum x1, blocking collectives, local(): gradient = lax.psum(gradients[0], 'grp') / lax.axis_size('grp')  36.2 us
  transfers between devices with their start and end apart: 5, of which 4 were waited for; matrix products, arithmetic and copies ran while one was open for 1% of the time, Pallas kernels for 0%

profile of v1, /device:TPU:2, one launch (start us, length us, event | category | flops | bytes accessed | tf_op | source)
XLA Modules:
  0.0 1561.2 jit_solution(12477456462300763490)
XLA Ops:
  7.2 0.0 copy-start.11
  7.2 0.0 all-gather.6.cloned.1.call-start
  7.2 36.2 %psum.21 = f32[16,512]{1,0:T(8,128)S(1)} all-reduce(f32[16,512]{1,0:T(8,128)} %bitcast.29), channel_id=1, replica_groups=mesh['grp'=8,'shard'=64] {'grp'}, use_global_device_ids=true, to_apply=%region_0.0 | all-reduce | flops 8192 | bytes 65536 | tf_op jit(solution)/shard_map/psum | solution.py:53
  43.4 0.8 convert_element_type.62
  44.3 1.4 fusion.34
  45.6 0.6 pad_maximum_fusion
  46.3 0.0 all-gather.6.cloned.1.call-update
  46.3 0.0 all-gather.8.cloned.1.call-start
  46.3 0.7 all-gather.8.cloned.1.call-update
  47.0 0.0 all-gather.12.cloned.1.call-start
  47.1 0.7 convert_element_type.66
  47.8 154.7 %all_gather.26 = bf16[512,512]{1,0:T(8,128)(2,1)S(1)} all-gather(bf16[8,512]{1,0:T(8,128)(2,1)S(1)} %convert_element_type.66), channel_id=1, replica_groups=mesh['grp'=8,'shard'=64] {'shard'}, dimensions={0}, use_global_device_ids=true | all-gather | bytes 532480 | tf_op jit(solution)/shard_map/all_gather | solution.py:58
  202.5 144.6 %all-gather.6.cloned.1.call-done = bf16[1024,1536]{1,0:T(8,128)(2,1)} async-done(((bf16[16,1536]{1,0:T(8,128)(2,1)}), bf16[1024,1536]{1,0:T(8,128)(2,1)}) %all-gather.6.cloned.1.call-update) | async-done | bytes 3145744 | tf_op jit(solution)/shard_map/all_gather | solution.py:61
  347.1 1.2 slice-done
  348.4 0.4 fusion.8
  348.8 0.3 multiply_reduce_fusion.1
  349.1 1.6 fusion.2
  350.7 0.0 copy-done
  350.8 0.0 copy-start.5
  350.8 0.9 multiply_reduce_fusion
  351.7 156.0 %all-reduce = (f32[1024]{0:T(1024)S(1)}, f32[512]{0:T(512)S(1)}) all-reduce(f32[1024]{0:T(1024)S(1)} %get-tuple-element.12, f32[512]{0:T(512)S(1)} %get-tuple-element.14), channel_id=1, replica_groups=mesh['grp'=8,'shard'=64] {'shard'}, use_global_device_ids=true, to_apply=%region_2.0 | all-reduce | flops 1536 | bytes 12288 | tf_op jit(solution)/shard_map/psum | solution.py:92
  507.7 0.6 divide_convert_fusion
  508.4 0.0 all-gather.12.cloned.1.call-update
  508.4 0.0 all-gather.10.cloned.1.call-start
  508.4 0.0 copy-start.1
  508.5 0.0 copy-start.9
  508.5 3.3 split.8
  511.7 135.3 %all-gather.8.cloned.1.call-done = bf16[1024,512]{1,0:T(8,128)(2,1)} async-done(((bf16[16,512]{1,0:T(8,128)(2,1)}), bf16[1024,512]{1,0:T(8,128)(2,1)}) %all-gather.8.cloned.1.call-update) | async-done | bytes 1048592 | tf_op jit(solution)/shard_map/all_gather | solution.py:72
  647.0 1.7 convolution_convert_fusion.3
  648.7 0.0 copy-done.1
  648.7 1.7 fusion.18
  650.4 2.2 convolution_convert_fusion.4
  652.6 0.0 all-gather.10.cloned.1.call-update
  652.6 0.0 all-gather.14.cloned.1.call-start
  652.7 296.9 %all-gather.12.cloned.1.call-done = bf16[1024,1024]{1,0:T(8,128)(2,1)} async-done(((bf16[16,1024]{1,0:T(8,128)(2,1)}), bf16[1024,1024]{1,0:T(8,128)(2,1)}) %all-gather.12.cloned.1.call-update) | async-done | bytes 2097168 | tf_op jit(solution)/shard_map/all_gather | solution.py:35
  949.5 0.0 copy-done.4
  949.5 3.8 fusion.3
  953.3 0.0 all-gather.14.cloned.1.call-update
  953.4 0.0 copy-start.3
  953.4 154.4 %all_gather.30 = bf16[512,512]{1,0:T(8,128)(2,1)S(1)} all-gather(bf16[8,512]{1,0:T(8,128)(2,1)S(1)} %divide_convert_fusion.1), channel_id=1, replica_groups=mesh['grp'=8,'shard'=64] {'shard'}, dimensions={0}, use_global_device_ids=true | all-gather | bytes 532480 | tf_op jit(solution)/shard_map/all_gather | solution.py:42
  1107.8 0.4 fusion.11
  1108.1 157.3 %all_gather.31 = bf16[512,512]{1,0:T(8,128)(2,1)S(1)} all-gather(bf16[8,512]{1,0:T(8,128)(2,1)S(1)} %fusion.11), channel_id=1, replica_groups=mesh['grp'=8,'shard'=64] {'shard'}, dimensions={0}, use_global_device_ids=true | all-gather | bytes 532480 | tf_op jit(solution)/shard_map/all_gather | solution.py:42
  1265.4 1.0 fusion.9
  1266.4 0.0 copy-done.10
  1266.5 2.1 fusion.5
  1268.6 282.4 %all-gather.14.cloned.1.call-done = bf16[1024,1024]{1,0:T(8,128)(2,1)} async-done(((bf16[16,1024]{1,0:T(8,128)(2,1)}), bf16[1024,1024]{1,0:T(8,128)(2,1)}) %all-gather.14.cloned.1.call-update) | async-done | bytes 2097168 | tf_op jit(solution)/shard_map/all_gather | solution.py:35
  1550.9 0.0 copy-done.3
  1550.9 3.8 fusion
  (19 shorter events, 0.1 us)
Async XLA Ops:
  7.2 340.0 %copy-start.11 = (f32[8,512]{1,0:T(8,128)S(1)}, f32[8,512]{1,0:T(8,128)}, u32[]{:S(2)}) copy-start(f32[8,512]{1,0:T(8,128)} %param.14) | copy-start | bytes 49156
  7.2 339.9 %all-gather.6.cloned.1.call-start = ((), (), s32[]{:S(2)}) async-start(), calls=%async_computation | async-start | bytes 3194880 | tf_op jit(solution)/shard_map/all_gather | solution.py:61
  46.3 600.7 %all-gather.8.cloned.1.call-start = ((), (), s32[]{:S(2)}) async-start(), calls=%async_computation.1 | async-start | bytes 1064960 | tf_op jit(solution)/shard_map/all_gather | solution.py:72
  47.0 902.5 %all-gather.12.cloned.1.call-start = ((), (), s32[]{:S(2)}) async-start(), calls=%async_computation.3 | async-start | bytes 2129920 | tf_op jit(solution)/shard_map/all_gather | solution.py:35
  47.8 301.3 %copy-start.8 = (f32[16,1024]{1,0:T(8,128)S(1)}, f32[16,1024]{1,0:T(8,128)}, u32[]{:S(2)}) copy-start(f32[16,1024]{1,0:T(8,128)} %param.12) | copy-start | bytes 196612
  202.5 148.2 %copy-start.2 = (bf16[512,512]{1,0:T(8,128)(2,1)}, bf16[512,512]{1,0:T(8,128)(2,1)S(1)}, u32[]{:S(2)}) copy-start(bf16[512,512]{1,0:T(8,128)(2,1)S(1)} %all_gather.26) | copy-start | bytes 1572868
  347.1 1.2 slice-start
  347.1 3.6 copy-start
  348.8 163.0 %copy-start.7 = (f32[8,512]{1,0:T(8,128)}, f32[8,512]{1,0:T(8,128)S(1)}, u32[]{:S(2)}) copy-start(f32[8,512]{1,0:T(8,128)S(1)} %fusion.8) | copy-start | bytes 49156
  350.8 161.0 %copy-start.5 = (f32[16,1024]{1,0:T(8,128)}, f32[16,1024]{1,0:T(8,128)S(1)}, u32[]{:S(2)}) copy-start(f32[16,1024]{1,0:T(8,128)S(1)} %fusion.2) | copy-start | bytes 196612
  508.4 758.1 %all-gather.10.cloned.1.call-start = ((), (), s32[]{:S(2)}) async-start(), calls=%async_computation.2 | async-start | bytes 1064960 | tf_op jit(solution)/shard_map/all_gather | solution.py:87
  508.4 140.3 %copy-start.1 = (bf16[1024,1536]{1,0:T(8,128)(2,1)S(1)}, bf16[1024,1536]{1,0:T(8,128)(2,1)}, u32[]{:S(2)}) copy-start(bf16[1024,1536]{1,0:T(8,128)(2,1)} %all-gather.6.cloned.1.call-done) | copy-start | bytes 9437188
  508.5 140.3 %copy-start.9 = (f32[16,512]{1,0:T(8,128)S(1)}, f32[16,512]{1,0:T(8,128)}, u32[]{:S(2)}) copy-start(f32[16,512]{1,0:T(8,128)} %param.11) | copy-start | bytes 98308
  511.7 437.8 %copy-start.4 = (bf16[16,1024]{1,0:T(8,128)(2,1)S(1)}, bf16[16,1024]{1,0:T(8,128)(2,1)}, u32[]{:S(2)}) copy-start(bf16[16,1024]{1,0:T(8,128)(2,1)} %divide_convert_fusion) | copy-start | bytes 98308
  650.4 302.9 %copy-start.6 = (f32[16,512]{1,0:T(8,128)}, f32[16,512]{1,0:T(8,128)S(1)}, u32[]{:S(2)}) copy-start(f32[16,512]{1,0:T(8,128)S(1)} %fusion.18) | copy-start | bytes 98308
  652.6 898.3 %all-gather.14.cloned.1.call-start = ((), (), s32[]{:S(2)}) async-start(), calls=%async_computation.4 | async-start | bytes 2129920 | tf_op jit(solution)/shard_map/all_gather | solution.py:35
  953.3 313.1 %copy-start.10 = (f32[16,512]{1,0:T(8,128)S(1)}, f32[16,512]{1,0:T(8,128)}, u32[]{:S(2)}) copy-start(f32[16,512]{1,0:T(8,128)} %param.9) | copy-start | bytes 98308
  953.4 597.5 %copy-start.3 = (bf16[16,1024]{1,0:T(8,128)(2,1)S(1)}, bf16[16,1024]{1,0:T(8,128)(2,1)}, u32[]{:S(2)}) copy-start(bf16[16,1024]{1,0:T(8,128)(2,1)} %fusion.3) | copy-start | bytes 98308
Sparse Core Ops, SparseCore 0:
  46.4 300.6 all-gather.5
  349.8 297.1 all-gather.7
  649.7 299.8 all-gather.11
  951.5 297.1 all-gather.9
  1251.1 299.7 all-gather.13
